TPU v7x, 32 devices: a whole 2x2x4 slice. The times are simulated.
32 devices in a mesh: grp: 2 (over x), row: 16 (over z, y, core).
Axes of the slice: x: 2, y: 2, z: 4, core: 2. Of those that a mesh axis runs over, the one named last changes fastest.
Arguments:
- latent: bfloat16 [4, 16, 48, 16], P('grp', 'row'), parts along dimension 0, may hold values from -70 to 70
- w_in: bfloat16 [27, 16, 512], replicated, may hold values from -0.3125 to 0.3125
- gain_in: float32 [512], replicated, may hold values from 0.25 to 1.75
- w_query: bfloat16 [512, 512], replicated, may hold values from -0.2298097 to 0.2298097
- w_key: bfloat16 [512, 512], replicated, may hold values from -1.45840774 to 1.45840774
- w_value: bfloat16 [512, 512], replicated, may hold values from -0.25 to 0.25
- w_out: bfloat16 [512, 512], replicated, may hold values from -0.25 to 0.25
- gain_up: float32 [512], replicated, may hold values from 0.25 to 1.75
- w_up: bfloat16 [27, 512, 512], P(None, 'row'), may hold values from -0.0546875 to 0.0546875
Outputs:
- decoded: bfloat16 [4, 32, 96, 512], P('grp', 'row'), parts along dimension 0
There are 2 independent parts, one for each index of `grp`. A program takes and returns all parts, laid end to end along the dimension named above; an argument that names none is the same for every part. Nothing has to cross between parts.
All inputs are finite; a program needn't handle non-finite values.
Results may differ from a plain program's by a relative error of at most 0.015.
Values may be sent and summed in bfloat16 or wider, within the bound.
No kernel may reach another device: no remote copies, remote signals or barrier semaphores. Data moves between devices by JAX's collectives and lax.ppermute only.
A program may use at most 128 MiB of HBM per device.

v0:
```python
import math
import jax
import jax.numpy as jnp
from jax import lax
from jax.sharding import PartitionSpec as P

GROUPS = 32
norm_eps = 1e-06


def extended(cells, sides, width):
    for axis, dim in sides:
        count = lax.axis_size(axis)
        ends = count - 1
        head = lax.slice_in_dim(cells, 0, width, axis=dim)
        tail = lax.slice_in_dim(cells, cells.shape[dim] - width, cells.shape[dim], axis=dim)
        cells = jnp.concatenate(
            [
                lax.ppermute(tail, axis, [(i, (i + 1) % count) for i in range(ends)]),
                cells,
                lax.ppermute(head, axis, [((i + 1) % count, i) for i in range(ends)]),
            ],
            axis=dim,
        )
    return cells


def pad_field(rimmed):
    spaced = jnp.pad(rimmed, ((0, 0), (0, 0), (1, 1), (0, 0)))
    first_frame = spaced[:1]
    return jnp.concatenate([first_frame, first_frame, spaced], axis=0)


def tap_windows(padded, frame_count, row_count, col_count):
    windows = []
    for frame_tap in range(3):
        for row_tap in range(3):
            for col_tap in range(3):
                windows.append(
                    padded[
                        frame_tap : frame_tap + frame_count,
                        row_tap : row_tap + row_count,
                        col_tap : col_tap + col_count,
                    ]
                )
    stacked = jnp.stack(windows, axis=3)
    return stacked.reshape(frame_count * row_count * col_count, -1)


def tap_products(padded, weight, frame_count, row_count, col_count):
    running = jnp.zeros((frame_count * row_count * col_count, weight.shape[2]), jnp.float32)
    for frame_tap in range(3):
        for row_tap in range(3):
            for col_tap in range(3):
                tap_index = (frame_tap * 3 + row_tap) * 3 + col_tap
                window = padded[
                    frame_tap : frame_tap + frame_count,
                    row_tap : row_tap + row_count,
                    col_tap : col_tap + col_count,
                ]
                window = window.reshape(frame_count * row_count * col_count, -1)
                running = running + jnp.dot(
                    window, weight[tap_index], preferred_element_type=jnp.float32
                )
    return running


def group_norm(volume, gain):
    grouped = volume.astype(jnp.float32).reshape(volume.shape[:3] + (GROUPS, -1))
    entry_count = (
        volume.shape[0]
        * volume.shape[1]
        * lax.axis_size("row")
        * volume.shape[2]
        * grouped.shape[4]
    )
    group_total = lax.psum(jnp.sum(grouped, axis=(0, 1, 2, 4)), "row")
    group_avg = group_total / entry_count
    centred = grouped - group_avg[:, None]
    variance = lax.psum(jnp.sum(centred * centred, axis=(0, 1, 2, 4)), "row") / entry_count
    normal_part = centred * lax.rsqrt(variance + norm_eps)[:, None]
    return normal_part.reshape(volume.shape) * gain


def per_device(latent, w_in, gain_in, w_query, w_key, w_value, w_out, gain_up, w_up):
    frame_count, row_count, col_count, _ = latent.shape
    chan_width = w_query.shape[0]
    rimmed = extended(latent, (("row", 1),), 1)
    first_out = jnp.dot(
        tap_windows(pad_field(rimmed), frame_count, row_count, col_count),
        w_in.reshape(-1, chan_width),
        preferred_element_type=jnp.float32,
    )
    first_out = first_out.astype(jnp.bfloat16).reshape(
        frame_count, row_count, col_count, chan_width
    )
    normed = group_norm(first_out, gain_in).astype(jnp.bfloat16)
    flat_rows = normed.reshape(-1, chan_width)
    queries = jnp.dot(flat_rows, w_query, preferred_element_type=jnp.float32).astype(jnp.bfloat16)
    queries = queries.reshape(frame_count, row_count * col_count, chan_width)
    score_scale = 1.0 / math.sqrt(chan_width)
    key_table = jnp.dot(flat_rows, w_key, preferred_element_type=jnp.float32).astype(jnp.bfloat16)
    value_table = jnp.dot(flat_rows, w_value, preferred_element_type=jnp.float32).astype(
        jnp.bfloat16
    )
    key_table = key_table.reshape(frame_count, row_count, col_count, chan_width)
    value_table = value_table.reshape(frame_count, row_count, col_count, chan_width)
    row_peak = jnp.full((frame_count, row_count * col_count), -jnp.inf, jnp.float32)
    denom = jnp.zeros((frame_count, row_count * col_count), jnp.float32)
    weighted = jnp.zeros((frame_count, row_count * col_count, chan_width), jnp.float32)
    scores = (
        jnp.einsum(
            "fqd,fkd->fqk",
            queries,
            lax.all_gather(key_table, "row", axis=1, tiled=True).reshape(
                frame_count, -1, chan_width
            ),
            preferred_element_type=jnp.float32,
        )
        * score_scale
    )
    new_peak = jnp.max(scores, axis=-1)
    correction = jnp.exp(row_peak - new_peak)
    expo = jnp.exp(scores - new_peak[..., None])
    denom = denom * correction + jnp.sum(expo, axis=-1)
    weighted = weighted * correction[..., None] + jnp.einsum(
        "fqk,fkd->fqd",
        expo.astype(jnp.bfloat16),
        lax.all_gather(value_table, "row", axis=1, tiled=True).reshape(frame_count, -1, chan_width),
        preferred_element_type=jnp.float32,
    )
    row_peak, denom, weighted = (new_peak, denom, weighted)
    attended = (weighted / denom[..., None]).astype(jnp.bfloat16).reshape(-1, chan_width)
    added = first_out.astype(jnp.float32).reshape(-1, chan_width) + jnp.dot(
        attended, w_out, preferred_element_type=jnp.float32
    )
    added = added.astype(jnp.bfloat16).reshape(frame_count, row_count, col_count, chan_width)
    full_up = lax.all_gather(w_up, "row", axis=1, tiled=True)
    upsampled = jnp.repeat(jnp.repeat(added, 2, axis=1), 2, axis=2)
    up_rimmed = extended(upsampled, (("row", 1),), 1)
    padded_up = pad_field(up_rimmed)
    running = tap_products(padded_up, full_up, frame_count, 2 * row_count, 2 * col_count)
    convolved = running.astype(jnp.bfloat16).reshape(
        frame_count, 2 * row_count, 2 * col_count, chan_width
    )
    return jax.nn.silu(group_norm(convolved, gain_up)).astype(jnp.bfloat16)


def solution(mesh):
    in_specs = (
        P("grp", "row", None, None),
        P(),
        P(),
        P(),
        P(),
        P(),
        P(),
        P(),
        P(None, "row", None),
    )
    out_specs = P("grp", "row", None, None)
    return jax.shard_map(
        per_device, mesh=mesh, in_specs=in_specs, out_specs=out_specs, check_vma=False
    )
```

profile of v0, /device:TPU:0, one launch (start us, length us, event | category | flops | bytes accessed | tf_op | source)
XLA Modules:
  0.0 361.8 jit_solution(4662353272731038480)
XLA Ops:
  6.5 1.4 collective-permute-start.1
  8.0 3.0 collective-permute-start
  16.7 35.5 %psum.28 = f32[32]{0:T(128)S(1)} all-reduce(f32[32]{0:T(128)S(1)} %reduce_sum.59), channel_id=1, replica_groups=mesh['grp'=2,'row'=16] {'row'}, use_global_device_ids=true, to_apply=%region_2.3 | all-reduce | flops 32 | bytes 256 | tf_op jit(solution)/shard_map/psum | solution.py:77
  52.5 29.5 %psum.29 = f32[32]{0:T(128)S(1)} all-reduce(f32[32]{0:T(128)S(1)} %reduce_sum.62), channel_id=1, replica_groups=mesh['grp'=2,'row'=16] {'row'}, use_global_device_ids=true, to_apply=%region_5.6 | all-reduce | flops 32 | bytes 256 | tf_op jit(solution)/shard_map/psum | solution.py:80
  83.9 1.9 convolution_convert_fusion.1
  86.5 1.3 convolution_convert_fusion.2
  87.8 33.0 %all-gather.6.cloned.1.call-done = bf16[2,16,48,512]{3,2,0,1:T(8,128)(2,1)} async-done(((bf16[2,1,48,512]{3,2,0,1:T(8,128)(2,1)}), bf16[2,16,48,512]{3,2,0,1:T(8,128)(2,1)}) %all-gather.6.cloned.1.call-update) | async-done | bytes 1572880 | tf_op jit(solution)/shard_map/all_gather | solution.py:129
  120.8 1.5 copy.34
  122.4 39.1 %all-gather.4.cloned.1.call-done = bf16[2,16,48,512]{3,2,0,1:T(8,128)(2,1)} async-done(((bf16[2,1,48,512]{3,2,0,1:T(8,128)(2,1)}), bf16[2,16,48,512]{3,2,0,1:T(8,128)(2,1)}) %all-gather.4.cloned.1.call-update) | async-done | bytes 1572880 | tf_op jit(solution)/shard_map/all_gather | solution.py:115
  161.5 1.5 copy.33
  164.7 1.3 collective-permute-start.3
  166.0 3.0 collective-permute-start.2
  170.5 2.1 pad_maximum_fusion.3
  173.6 2.3 pad_maximum_fusion.2
  175.9 97.0 %all-gather.8.cloned.1.call-done = bf16[27,512,512]{2,1,0:T(8,128)(2,1)} async-done(((bf16[27,32,512]{2,1,0:T(8,128)(2,1)}), bf16[27,512,512]{2,1,0:T(8,128)(2,1)}) %all-gather.8.cloned.1.call-update) | async-done | bytes 14155792 | tf_op jit(solution)/shard_map/all_gather | solution.py:138
  273.0 1.7 fusion.12
  274.7 2.2 convolution_add_fusion.25
  276.9 2.3 convolution_add_fusion.24
  279.2 1.6 convolution_add_fusion.23
  280.8 1.6 convolution_add_fusion.22
  282.4 1.6 convolution_add_fusion.21
  284.0 1.4 convolution_add_fusion.20
  293.3 30.8 %psum.30 = f32[32]{0:T(128)S(1)} all-reduce(f32[32]{0:T(128)S(1)} %reduce_sum.82), channel_id=1, replica_groups=mesh['grp'=2,'row'=16] {'row'}, use_global_device_ids=true, to_apply=%region_10.11 | all-reduce | flops 32 | bytes 256 | tf_op jit(solution)/shard_map/psum | solution.py:77
  324.6 29.5 %psum.31 = f32[32]{0:T(128)S(1)} all-reduce(f32[32]{0:T(128)S(1)} %reduce_sum.85), channel_id=1, replica_groups=mesh['grp'=2,'row'=16] {'row'}, use_global_device_ids=true, to_apply=%region_13.14 | all-reduce | flops 32 | bytes 256 | tf_op jit(solution)/shard_map/psum | solution.py:80
  (134 shorter events, 21.9 us)
Async XLA Ops:
  6.5 76.4 %copy-start = (bf16[512,512]{1,0:T(8,128)(2,1)S(1)}, bf16[512,512]{1,0:T(8,128)(2,1)}, u32[]{:S(2)}) copy-start(bf16[512,512]{1,0:T(8,128)(2,1)} %param.14) | copy-start | bytes 1572868
  6.5 157.8 %copy-start.15 = (bf16[512,512]{1,0:T(8,128)(2,1)S(1)}, bf16[512,512]{1,0:T(8,128)(2,1)}, u32[]{:S(2)}) copy-start(bf16[512,512]{1,0:T(8,128)(2,1)} %param.15) | copy-start | bytes 1572868
  6.5 114.3 %all-gather.6.cloned.1.call-start = ((), (), s32[]{:S(2)}) async-start(), calls=%async_computation.1 | async-start | bytes 1671168 | tf_op jit(solution)/shard_map/all_gather | solution.py:129
  6.5 4.5 %collective-permute-start.1 = (bf16[2,1,48,16]{2,3,1,0:T(8,128)(2,1)}, bf16[2,1,48,16]{2,3,1,0:T(8,128)(2,1)S(1)}, u32[]{:S(2)}, u32[]{:S(2)}) collective-permute-start(bf16[2,1,48,16]{2,3,1,0:T(8,128)(2,1)} %param.9), channel_id=1, source_target_pairs={{1,0},{2,1},{3,2},{4,3},{5,4},{6,5},{7,6},{8,7},{9,8},{10,9},{11,1... | collective-permute-start | bytes 9224 | tf_op jit(solution)/shard_map/ppermute | solution.py:21
  8.0 4.1 %collective-permute-start = (bf16[2,1,48,16]{2,3,0,1:T(8,128)(2,1)}, bf16[2,1,48,16]{2,3,0,1:T(8,128)(2,1)S(1)}, u32[]{:S(2)}, u32[]{:S(2)}) collective-permute-start(bf16[2,1,48,16]{2,3,0,1:T(8,128)(2,1)} %bitcast.310), channel_id=1, source_target_pairs={{0,1},{1,2},{2,3},{3,4},{4,5},{5,6},{6,7},{7,8},{8,9},{9,10},{10,1... | collective-permute-start | bytes 9224 | tf_op jit(solution)/shard_map/ppermute | solution.py:19
  83.8 77.6 %all-gather.4.cloned.1.call-start = ((), (), s32[]{:S(2)}) async-start(), calls=%async_computation | async-start | bytes 1671168 | tf_op jit(solution)/shard_map/all_gather | solution.py:115
  85.8 187.1 %all-gather.8.cloned.1.call-start = ((), (), s32[]{:S(2)}) async-start(), calls=%async_computation.2 | async-start | bytes 15040512 | tf_op jit(solution)/shard_map/all_gather | solution.py:138
  164.7 4.4 %collective-permute-start.3 = (bf16[2,1,96,512]{3,2,0,1:T(8,128)(2,1)S(1)}, bf16[2,1,96,512]{3,2,0,1:T(8,128)(2,1)S(1)}, u32[]{:S(2)}, u32[]{:S(2)}) collective-permute-start(bf16[2,1,96,512]{3,2,0,1:T(8,128)(2,1)S(1)} %slice.314), channel_id=1, source_target_pairs={{1,0},{2,1},{3,2},{4,3},{5,4},{6,5},{7,6},{8,7},{9,8},{10,9},{11,1... | collective-permute-start | bytes 589832 | tf_op jit(solution)/shard_map/ppermute | solution.py:21
  166.0 4.1 %collective-permute-start.2 = (bf16[2,1,96,512]{3,2,0,1:T(8,128)(2,1)S(1)}, bf16[2,1,96,512]{3,2,0,1:T(8,128)(2,1)S(1)}, u32[]{:S(2)}, u32[]{:S(2)}) collective-permute-start(bf16[2,1,96,512]{3,2,0,1:T(8,128)(2,1)S(1)} %slice.314), channel_id=1, source_target_pairs={{0,1},{1,2},{2,3},{3,4},{4,5},{5,6},{6,7},{7,8},{8,9},{9,10},{10,1... | collective-permute-start | bytes 589832 | tf_op jit(solution)/shard_map/ppermute | solution.py:19
  272.9 11.1 %copy-start.1 = (bf16[27,512,512]{2,1,0:T(8,128)(2,1)S(1)}, bf16[27,512,512]{2,1,0:T(8,128)(2,1)}, u32[]{:S(2)}) copy-start(bf16[27,512,512]{2,1,0:T(8,128)(2,1)} %all-gather.8.cloned.1.call-done) | copy-start | bytes 42467332
  272.9 12.5 %copy-start.11 = (bf16[2,2,96,512]{3,2,1,0:T(8,128)(2,1)S(1)}, bf16[2,2,96,512]{3,2,1,0:T(8,128)(2,1)}, u32[]{:S(2)}) copy-start(bf16[2,2,96,512]{3,2,1,0:T(8,128)(2,1)} %get-tuple-element.27) | copy-start | bytes 1179652
  272.9 12.9 %copy-start.9 = (bf16[2,2,96,512]{3,2,1,0:T(8,128)(2,1)S(1)}, bf16[2,2,96,512]{3,2,1,0:T(8,128)(2,1)}, u32[]{:S(2)}) copy-start(bf16[2,2,96,512]{3,2,1,0:T(8,128)(2,1)} %get-tuple-element.20) | copy-start | bytes 1179652
  273.0 13.3 %copy-start.13 = (bf16[2,2,96,512]{3,2,1,0:T(8,128)(2,1)S(1)}, bf16[2,2,96,512]{3,2,1,0:T(8,128)(2,1)}, u32[]{:S(2)}) copy-start(bf16[2,2,96,512]{3,2,1,0:T(8,128)(2,1)} %get-tuple-element.6) | copy-start | bytes 1179652
  273.0 13.7 %copy-start.12 = (bf16[2,2,96,512]{3,2,1,0:T(8,128)(2,1)S(1)}, bf16[2,2,96,512]{3,2,1,0:T(8,128)(2,1)}, u32[]{:S(2)}) copy-start(bf16[2,2,96,512]{3,2,1,0:T(8,128)(2,1)} %get-tuple-element.7) | copy-start | bytes 1179652
  273.0 14.0 %copy-start.10 = (bf16[2,2,96,512]{3,2,1,0:T(8,128)(2,1)S(1)}, bf16[2,2,96,512]{3,2,1,0:T(8,128)(2,1)}, u32[]{:S(2)}) copy-start(bf16[2,2,96,512]{3,2,1,0:T(8,128)(2,1)} %get-tuple-element.8) | copy-start | bytes 1179652
  273.0 14.4 %copy-start.8 = (bf16[2,2,96,512]{3,2,1,0:T(8,128)(2,1)S(1)}, bf16[2,2,96,512]{3,2,1,0:T(8,128)(2,1)}, u32[]{:S(2)}) copy-start(bf16[2,2,96,512]{3,2,1,0:T(8,128)(2,1)} %get-tuple-element.9) | copy-start | bytes 1179652
  276.9 10.9 %copy-start.7 = (bf16[2,2,96,512]{3,2,1,0:T(8,128)(2,1)S(1)}, bf16[2,2,96,512]{3,2,1,0:T(8,128)(2,1)}, u32[]{:S(2)}) copy-start(bf16[2,2,96,512]{3,2,1,0:T(8,128)(2,1)} %get-tuple-element.10) | copy-start | bytes 1179652
  279.2 8.9 %copy-start.6 = (bf16[2,2,96,512]{3,2,1,0:T(8,128)(2,1)S(1)}, bf16[2,2,96,512]{3,2,1,0:T(8,128)(2,1)}, u32[]{:S(2)}) copy-start(bf16[2,2,96,512]{3,2,1,0:T(8,128)(2,1)} %get-tuple-element.11) | copy-start | bytes 1179652
  280.8 7.7 %copy-start.5 = (bf16[2,2,96,512]{3,2,1,0:T(8,128)(2,1)S(1)}, bf16[2,2,96,512]{3,2,1,0:T(8,128)(2,1)}, u32[]{:S(2)}) copy-start(bf16[2,2,96,512]{3,2,1,0:T(8,128)(2,1)} %get-tuple-element.12) | copy-start | bytes 1179652
  282.4 6.5 %copy-start.4 = (bf16[2,2,96,512]{3,2,1,0:T(8,128)(2,1)S(1)}, bf16[2,2,96,512]{3,2,1,0:T(8,128)(2,1)}, u32[]{:S(2)}) copy-start(bf16[2,2,96,512]{3,2,1,0:T(8,128)(2,1)} %get-tuple-element.13) | copy-start | bytes 1179652
  284.0 5.3 %copy-start.3 = (bf16[2,2,96,512]{3,2,1,0:T(8,128)(2,1)S(1)}, bf16[2,2,96,512]{3,2,1,0:T(8,128)(2,1)}, u32[]{:S(2)}) copy-start(bf16[2,2,96,512]{3,2,1,0:T(8,128)(2,1)} %get-tuple-element.5) | copy-start | bytes 1179652
  285.5 4.3 %copy-start.2 = (bf16[2,2,96,512]{3,2,1,0:T(8,128)(2,1)S(1)}, bf16[2,2,96,512]{3,2,1,0:T(8,128)(2,1)}, u32[]{:S(2)}) copy-start(bf16[2,2,96,512]{3,2,1,0:T(8,128)(2,1)} %get-tuple-element.19) | copy-start | bytes 1179652
  288.5 4.2 %copy-start.14 = (bf16[2,2,96,512]{3,2,1,0:T(8,128)(2,1)S(1)}, bf16[2,2,96,512]{3,2,1,0:T(8,128)(2,1)}, u32[]{:S(2)}) copy-start(bf16[2,2,96,512]{3,2,1,0:T(8,128)(2,1)} %get-tuple-element.14) | copy-start | bytes 1179652
  288.9 65.4 %copy-start.16 = (f32[512]{0:T(512)S(1)}, f32[512]{0:T(512)}, u32[]{:S(2)}) copy-start(f32[512]{0:T(512)} %param.16) | copy-start | bytes 6148
Sparse Core Ops, SparseCore 0:
  83.9 36.8 all-gather.5
  123.1 38.2 all-gather.3
  163.7 109.2 all-gather.7
where the time goes:
time: 362 us
  waiting for transfers between devices  172 us (48%)
  blocking collectives  125 us (35%)
  matrix products  26.3 us (7%)
  between operations  13.7 us (4%)
  other arithmetic  9.18 us (3%)
  starting transfers between devices  8.87 us (2%)
  local copies, waits for them, and re-layouts  6.63 us (2%)
    all_gather x1, waiting for transfers between devices, per_device(): full_up = lax.all_gather(w_up, 'row', axis=1, tiled=True)  97 us
    psum x2, blocking collectives, group_norm(): group_total = lax.psum(jnp.sum(grouped, axis=(0, 1, 2, 4)), 'row')  66.3 us
    psum x2, blocking collectives, group_norm(): lax.psum(jnp.sum(centred * centred, axis=(0, 1, 2, 4)), 'row') / entry_count  59 us
    all_gather x1, waiting for transfers between devices, per_device(): lax.all_gather(key_table, 'row', axis=1, tiled=True)  39.1 us
    all_gather x1, waiting for transfers between devices, per_device(): lax.all_gather(value_table, 'row', axis=1, tiled=True)  33 us
    dot_general x27, matrix products, tap_products(): jnp.dot(window, weight[tap_index], preferred_element_type=jnp.float32)  19.7 us
  transfers between devices with their start and end apart: 7, of which 5 were waited for; matrix products, arithmetic and copies ran while one was open for 4% of the time, Pallas kernels for 0%

commit v1 on v0

--- a/solution.py
+++ b/solution.py
@@ -6,6 +6,19 @@
 
 GROUPS = 32
 norm_eps = 1e-06
+
+
+def ring_gather(x, axis, dim):
+    ways = lax.axis_size(axis)
+    up = [(d, (d + 1) % ways) for d in range(ways)]
+    down = [(d, (d - 1) % ways) for d in range(ways)]
+    earlier, later = ([x], [x])
+    for _ in range(ways // 2):
+        earlier.append(lax.ppermute(earlier[-1], axis, up))
+    for _ in range((ways - 1) // 2):
+        later.append(lax.ppermute(later[-1], axis, down))
+    line = jnp.concatenate([*earlier[::-1], *later[1:]], axis=dim)
+    return jnp.roll(line, (lax.axis_index(axis) - ways // 2) * x.shape[dim], axis=dim)
 
 
 def extended(cells, sides, width):
@@ -126,7 +139,7 @@
     weighted = weighted * correction[..., None] + jnp.einsum(
         "fqk,fkd->fqd",
         expo.astype(jnp.bfloat16),
-        lax.all_gather(value_table, "row", axis=1, tiled=True).reshape(frame_count, -1, chan_width),
+        ring_gather(value_table, "row", 1).reshape(frame_count, -1, chan_width),
         preferred_element_type=jnp.float32,
     )
     row_peak, denom, weighted = (new_peak, denom, weighted)

time: 362 us -> 325 us (0.90)
  waiting for transfers between devices: 172 us -> 107 us
  starting transfers between devices: 8.87 us -> 40.5 us
    all_gather x1, waiting for transfers between devices: 39.1 us -> 0.02 us  [per_device(): lax.all_gather(key_table, 'row', axis=1, tiled=True)]
    all_gather x1 -> x0, waiting for transfers between devices: 33 us -> none  [per_device(): lax.all_gather(value_table, 'row', axis=1, tiled=True)]
    ppermute x0 -> x15, starting transfers between devices: none -> 31.5 us  [the longest x7 31.5 us: ring_gather(): later.append(lax.ppermute(later[-1], axis, down))]
    ppermute x0 -> x15, waiting for transfers between devices: none -> 29.1 us  [the longest x8 26 us: ring_gather(): earlier.append(lax.ppermute(earlier[-1], axis, up))]
    all_gather x1, waiting for transfers between devices: 97 us -> 75.1 us  [per_device(): full_up = lax.all_gather(w_up, 'row', axis=1, tiled=True)]
  transfers between devices with their start and end apart: 7 -> 21, of which waited for: 5 -> 13; matrix products, arithmetic and copies ran while one was open for 4% -> 3% of each run, Pallas kernels for 0% -> 0%
where the time goes in v1:
time: 325 us
  blocking collectives  125 us (38%)
  waiting for transfers between devices  107 us (33%)
  starting transfers between devices  40.5 us (12%)
  matrix products  22.9 us (7%)
  between operations  14.4 us (4%)
  other arithmetic  9.19 us (3%)
  local copies, waits for them, and re-layouts  5.75 us (2%)
    all_gather x1, waiting for transfers between devices, per_device(): full_up = lax.all_gather(w_up, 'row', axis=1, tiled=True)  75.1 us
    psum x2, blocking collectives, group_norm(): group_total = lax.psum(jnp.sum(grouped, axis=(0, 1, 2, 4)), 'row')  66.3 us
    psum x2, blocking collectives, group_norm(): lax.psum(jnp.sum(centred * centred, axis=(0, 1, 2, 4)), 'row') / entry_count  59 us
    ppermute x7, starting transfers between devices, ring_gather(): later.append(lax.ppermute(later[-1], axis, down))  31.5 us
    ppermute x8, waiting for transfers between devices, ring_gather(): earlier.append(lax.ppermute(earlier[-1], axis, up))  26 us
    dot_general x27, matrix products, tap_products(): jnp.dot(window, weight[tap_index], preferred_element_type=jnp.float32)  19.1 us
  transfers between devices with their start and end apart: 21, of which 13 were waited for; matrix products, arithmetic and copies ran while one was open for 3% of the time, Pallas kernels for 0%

profile of v1, /device:TPU:0, one launch (start us, length us, event | category | flops | bytes accessed | tf_op | source)
XLA Modules:
  0.0 324.8 jit_solution(5126789945253491930)
XLA Ops:
  8.0 3.0 collective-permute-start
  16.7 35.5 %psum.28 = f32[32]{0:T(128)S(1)} all-reduce(f32[32]{0:T(128)S(1)} %reduce_sum.59), channel_id=1, replica_groups=mesh['grp'=2,'row'=16] {'row'}, use_global_device_ids=true, to_apply=%region_2.3 | all-reduce | flops 32 | bytes 256 | tf_op jit(solution)/shard_map/psum | solution.py:90
  52.6 29.5 %psum.29 = f32[32]{0:T(128)S(1)} all-reduce(f32[32]{0:T(128)S(1)} %reduce_sum.62), channel_id=1, replica_groups=mesh['grp'=2,'row'=16] {'row'}, use_global_device_ids=true, to_apply=%region_5.6 | all-reduce | flops 32 | bytes 256 | tf_op jit(solution)/shard_map/psum | solution.py:93
  84.9 6.7 %collective-permute-done.2 = bf16[2,1,48,512]{3,2,0,1:T(8,128)(2,1)S(1)} collective-permute-done((bf16[2,1,48,512]{3,2,0,1:T(8,128)(2,1)S(1)}, bf16[2,1,48,512]{3,2,0,1:T(8,128)(2,1)S(1)}, u32[]{:S(2)}, u32[]{:S(2)}) %collective-permute-start.2) | collective-permute-done | bytes 98336 | tf_op jit(solution)/shard_map/ppermute | solution.py:17
  91.6 4.4 %collective-permute-start.10 = (bf16[2,1,48,512]{3,2,0,1:T(8,128)(2,1)S(1)}, bf16[2,1,48,512]{3,2,0,1:T(8,128)(2,1)S(1)}, u32[]{:S(2)}, u32[]{:S(2)}) collective-permute-start(bf16[2,1,48,512]{3,2,0,1:T(8,128)(2,1)S(1)} %bitcast.301), channel_id=1, source_target_pairs={{0,15},{1,0},{2,1},{3,2},{4,3},{5,4},{6,5},{7,6},{8,7},{9,8},{10,9... | collective-permute-start | bytes 294920 | tf_op jit(solution)/shard_map/ppermute | solution.py:19
  96.1 3.1 collective-permute-done.3
  99.2 4.4 %collective-permute-start.11 = (bf16[2,1,48,512]{3,2,0,1:T(8,128)(2,1)S(1)}, bf16[2,1,48,512]{3,2,0,1:T(8,128)(2,1)S(1)}, u32[]{:S(2)}, u32[]{:S(2)}) collective-permute-start(bf16[2,1,48,512]{3,2,0,1:T(8,128)(2,1)S(1)} %collective-permute-done.10), channel_id=1, source_target_pairs={{0,15},{1,0},{2,1},{3,2},{4,3},{5,4},{6,5},{7,6},{8,7},{9,8},{10,9... | collective-permute-start | bytes 294920 | tf_op jit(solution)/shard_map/ppermute | solution.py:19
  103.7 2.3 collective-permute-done.4
  106.0 4.5 %collective-permute-start.12 = (bf16[2,1,48,512]{3,2,0,1:T(8,128)(2,1)S(1)}, bf16[2,1,48,512]{3,2,0,1:T(8,128)(2,1)S(1)}, u32[]{:S(2)}, u32[]{:S(2)}) collective-permute-start(bf16[2,1,48,512]{3,2,0,1:T(8,128)(2,1)S(1)} %collective-permute-done.11), channel_id=1, source_target_pairs={{0,15},{1,0},{2,1},{3,2},{4,3},{5,4},{6,5},{7,6},{8,7},{9,8},{10,9... | collective-permute-start | bytes 294920 | tf_op jit(solution)/shard_map/ppermute | solution.py:19
  110.5 4.2 %collective-permute-done.5 = bf16[2,1,48,512]{3,2,0,1:T(8,128)(2,1)S(1)} collective-permute-done((bf16[2,1,48,512]{3,2,0,1:T(8,128)(2,1)S(1)}, bf16[2,1,48,512]{3,2,0,1:T(8,128)(2,1)S(1)}, u32[]{:S(2)}, u32[]{:S(2)}) %collective-permute-start.5) | collective-permute-done | bytes 98336 | tf_op jit(solution)/shard_map/ppermute | solution.py:17
  114.7 4.4 %collective-permute-start.13 = (bf16[2,1,48,512]{3,2,0,1:T(8,128)(2,1)S(1)}, bf16[2,1,48,512]{3,2,0,1:T(8,128)(2,1)S(1)}, u32[]{:S(2)}, u32[]{:S(2)}) collective-permute-start(bf16[2,1,48,512]{3,2,0,1:T(8,128)(2,1)S(1)} %collective-permute-done.12), channel_id=1, source_target_pairs={{0,15},{1,0},{2,1},{3,2},{4,3},{5,4},{6,5},{7,6},{8,7},{9,8},{10,9... | collective-permute-start | bytes 294920 | tf_op jit(solution)/shard_map/ppermute | solution.py:19
  119.1 2.5 collective-permute-done.6
  121.6 4.4 %collective-permute-start.14 = (bf16[2,1,48,512]{3,2,0,1:T(8,128)(2,1)S(1)}, bf16[2,1,48,512]{3,2,0,1:T(8,128)(2,1)S(1)}, u32[]{:S(2)}, u32[]{:S(2)}) collective-permute-start(bf16[2,1,48,512]{3,2,0,1:T(8,128)(2,1)S(1)} %collective-permute-done.13), channel_id=1, source_target_pairs={{0,15},{1,0},{2,1},{3,2},{4,3},{5,4},{6,5},{7,6},{8,7},{9,8},{10,9... | collective-permute-start | bytes 294920 | tf_op jit(solution)/shard_map/ppermute | solution.py:19
  126.0 2.3 collective-permute-done.7
  128.3 4.5 %collective-permute-start.15 = (bf16[2,1,48,512]{3,2,0,1:T(8,128)(2,1)S(1)}, bf16[2,1,48,512]{3,2,0,1:T(8,128)(2,1)S(1)}, u32[]{:S(2)}, u32[]{:S(2)}) collective-permute-start(bf16[2,1,48,512]{3,2,0,1:T(8,128)(2,1)S(1)} %collective-permute-done.14), channel_id=1, source_target_pairs={{0,15},{1,0},{2,1},{3,2},{4,3},{5,4},{6,5},{7,6},{8,7},{9,8},{10,9... | collective-permute-start | bytes 294920 | tf_op jit(solution)/shard_map/ppermute | solution.py:19
  132.9 2.3 collective-permute-done.8
  137.0 4.6 %collective-permute-start.16 = (bf16[2,1,48,512]{3,2,0,1:T(8,128)(2,1)S(1)}, bf16[2,1,48,512]{3,2,0,1:T(8,128)(2,1)S(1)}, u32[]{:S(2)}, u32[]{:S(2)}) collective-permute-start(bf16[2,1,48,512]{3,2,0,1:T(8,128)(2,1)S(1)} %collective-permute-done.15), channel_id=1, source_target_pairs={{0,15},{1,0},{2,1},{3,2},{4,3},{5,4},{6,5},{7,6},{8,7},{9,8},{10,9... | collective-permute-start | bytes 294920 | tf_op jit(solution)/shard_map/ppermute | solution.py:19
  141.6 2.6 collective-permute-done.9
  151.2 3.2 collective-permute-start.17
  155.7 2.1 pad_maximum_fusion.3
  158.7 2.4 pad_maximum_fusion.2
  161.1 75.1 %all-gather.5.cloned.1.call-done = bf16[27,512,512]{2,1,0:T(8,128)(2,1)} async-done(((bf16[27,32,512]{2,1,0:T(8,128)(2,1)}), bf16[27,512,512]{2,1,0:T(8,128)(2,1)}) %all-gather.5.cloned.1.call-update) | async-done | bytes 14155792 | tf_op jit(solution)/shard_map/all_gather | solution.py:151
  256.0 30.8 %psum.30 = f32[32]{0:T(128)S(1)} all-reduce(f32[32]{0:T(128)S(1)} %reduce_sum.82), channel_id=1, replica_groups=mesh['grp'=2,'row'=16] {'row'}, use_global_device_ids=true, to_apply=%region_10.11 | all-reduce | flops 32 | bytes 256 | tf_op jit(solution)/shard_map/psum | solution.py:90
  287.3 29.5 %psum.31 = f32[32]{0:T(128)S(1)} all-reduce(f32[32]{0:T(128)S(1)} %reduce_sum.85), channel_id=1, replica_groups=mesh['grp'=2,'row'=16] {'row'}, use_global_device_ids=true, to_apply=%region_13.14 | all-reduce | flops 32 | bytes 256 | tf_op jit(solution)/shard_map/psum | solution.py:93
  (198 shorter events, 41.9 us)
Async XLA Ops:
  6.5 76.4 %copy-start = (bf16[512,512]{1,0:T(8,128)(2,1)S(1)}, bf16[512,512]{1,0:T(8,128)(2,1)}, u32[]{:S(2)}) copy-start(bf16[512,512]{1,0:T(8,128)(2,1)} %param.13) | copy-start | bytes 1572868
  6.5 78.1 %copy-start.16 = (bf16[512,512]{1,0:T(8,128)(2,1)S(1)}, bf16[512,512]{1,0:T(8,128)(2,1)}, u32[]{:S(2)}) copy-start(bf16[512,512]{1,0:T(8,128)(2,1)} %param.14) | copy-start | bytes 1572868
  6.5 128.6 %copy-start.17 = (bf16[512,512]{1,0:T(8,128)(2,1)S(1)}, bf16[512,512]{1,0:T(8,128)(2,1)}, u32[]{:S(2)}) copy-start(bf16[512,512]{1,0:T(8,128)(2,1)} %param.12) | copy-start | bytes 1572868
  6.5 140.0 %all-gather.3.cloned.1.call-start = ((), (), s32[]{:S(2)}) async-start(), calls=%async_computation | async-start | bytes 1671168 | tf_op jit(solution)/shard_map/all_gather | solution.py:128
  6.5 4.5 %collective-permute-start.1 = (bf16[2,1,48,16]{2,3,1,0:T(8,128)(2,1)}, bf16[2,1,48,16]{2,3,1,0:T(8,128)(2,1)S(1)}, u32[]{:S(2)}, u32[]{:S(2)}) collective-permute-start(bf16[2,1,48,16]{2,3,1,0:T(8,128)(2,1)} %param.9), channel_id=1, source_target_pairs={{1,0},{2,1},{3,2},{4,3},{5,4},{6,5},{7,6},{8,7},{9,8},{10,9},{11,1... | collective-permute-start | bytes 9224 | tf_op jit(solution)/shard_map/ppermute | solution.py:34
  8.0 4.1 %collective-permute-start = (bf16[2,1,48,16]{2,3,0,1:T(8,128)(2,1)}, bf16[2,1,48,16]{2,3,0,1:T(8,128)(2,1)S(1)}, u32[]{:S(2)}, u32[]{:S(2)}) collective-permute-start(bf16[2,1,48,16]{2,3,0,1:T(8,128)(2,1)} %bitcast.313), channel_id=1, source_target_pairs={{0,1},{1,2},{2,3},{3,4},{4,5},{5,6},{6,7},{7,8},{8,9},{9,10},{10,1... | collective-permute-start | bytes 9224 | tf_op jit(solution)/shard_map/ppermute | solution.py:32
  83.8 152.4 %all-gather.5.cloned.1.call-start = ((), (), s32[]{:S(2)}) async-start(), calls=%async_computation.1 | async-start | bytes 15040512 | tf_op jit(solution)/shard_map/all_gather | solution.py:151
  84.8 6.8 %collective-permute-start.2 = (bf16[2,1,48,512]{3,2,0,1:T(8,128)(2,1)S(1)}, bf16[2,1,48,512]{3,2,0,1:T(8,128)(2,1)S(1)}, u32[]{:S(2)}, u32[]{:S(2)}) collective-permute-start(bf16[2,1,48,512]{3,2,0,1:T(8,128)(2,1)S(1)} %bitcast.300), channel_id=1, source_target_pairs={{0,1},{1,2},{2,3},{3,4},{4,5},{5,6},{6,7},{7,8},{8,9},{9,10},{10,1... | collective-permute-start | bytes 294920 | tf_op jit(solution)/shard_map/ppermute | solution.py:17
  91.6 7.6 %collective-permute-start.3 = (bf16[2,1,48,512]{3,2,0,1:T(8,128)(2,1)S(1)}, bf16[2,1,48,512]{3,2,0,1:T(8,128)(2,1)S(1)}, u32[]{:S(2)}, u32[]{:S(2)}) collective-permute-start(bf16[2,1,48,512]{3,2,0,1:T(8,128)(2,1)S(1)} %collective-permute-done.2), channel_id=1, source_target_pairs={{0,1},{1,2},{2,3},{3,4},{4,5},{5,6},{6,7},{7,8},{8,9},{9,10},{10,1... | collective-permute-start | bytes 294920 | tf_op jit(solution)/shard_map/ppermute | solution.py:17
  91.6 7.6 %collective-permute-start.10 = (bf16[2,1,48,512]{3,2,0,1:T(8,128)(2,1)S(1)}, bf16[2,1,48,512]{3,2,0,1:T(8,128)(2,1)S(1)}, u32[]{:S(2)}, u32[]{:S(2)}) collective-permute-start(bf16[2,1,48,512]{3,2,0,1:T(8,128)(2,1)S(1)} %bitcast.301), channel_id=1, source_target_pairs={{0,15},{1,0},{2,1},{3,2},{4,3},{5,4},{6,5},{7,6},{8,7},{9,8},{10,9... | collective-permute-start | bytes 294920 | tf_op jit(solution)/shard_map/ppermute | solution.py:19
  99.2 6.7 %collective-permute-start.4 = (bf16[2,1,48,512]{3,2,0,1:T(8,128)(2,1)S(1)}, bf16[2,1,48,512]{3,2,0,1:T(8,128)(2,1)S(1)}, u32[]{:S(2)}, u32[]{:S(2)}) collective-permute-start(bf16[2,1,48,512]{3,2,0,1:T(8,128)(2,1)S(1)} %collective-permute-done.3), channel_id=1, source_target_pairs={{0,1},{1,2},{2,3},{3,4},{4,5},{5,6},{6,7},{7,8},{8,9},{9,10},{10,1... | collective-permute-start | bytes 294920 | tf_op jit(solution)/shard_map/ppermute | solution.py:17
  99.2 6.7 %collective-permute-start.11 = (bf16[2,1,48,512]{3,2,0,1:T(8,128)(2,1)S(1)}, bf16[2,1,48,512]{3,2,0,1:T(8,128)(2,1)S(1)}, u32[]{:S(2)}, u32[]{:S(2)}) collective-permute-start(bf16[2,1,48,512]{3,2,0,1:T(8,128)(2,1)S(1)} %collective-permute-done.10), channel_id=1, source_target_pairs={{0,15},{1,0},{2,1},{3,2},{4,3},{5,4},{6,5},{7,6},{8,7},{9,8},{10,9... | collective-permute-start | bytes 294920 | tf_op jit(solution)/shard_map/ppermute | solution.py:19
  105.9 8.7 %collective-permute-start.5 = (bf16[2,1,48,512]{3,2,0,1:T(8,128)(2,1)S(1)}, bf16[2,1,48,512]{3,2,0,1:T(8,128)(2,1)S(1)}, u32[]{:S(2)}, u32[]{:S(2)}) collective-permute-start(bf16[2,1,48,512]{3,2,0,1:T(8,128)(2,1)S(1)} %collective-permute-done.4), channel_id=1, source_target_pairs={{0,1},{1,2},{2,3},{3,4},{4,5},{5,6},{6,7},{7,8},{8,9},{9,10},{10,1... | collective-permute-start | bytes 294920 | tf_op jit(solution)/shard_map/ppermute | solution.py:17
  106.0 8.7 %collective-permute-start.12 = (bf16[2,1,48,512]{3,2,0,1:T(8,128)(2,1)S(1)}, bf16[2,1,48,512]{3,2,0,1:T(8,128)(2,1)S(1)}, u32[]{:S(2)}, u32[]{:S(2)}) collective-permute-start(bf16[2,1,48,512]{3,2,0,1:T(8,128)(2,1)S(1)} %collective-permute-done.11), channel_id=1, source_target_pairs={{0,15},{1,0},{2,1},{3,2},{4,3},{5,4},{6,5},{7,6},{8,7},{9,8},{10,9... | collective-permute-start | bytes 294920 | tf_op jit(solution)/shard_map/ppermute | solution.py:19
  114.6 6.9 %collective-permute-start.6 = (bf16[2,1,48,512]{3,2,0,1:T(8,128)(2,1)S(1)}, bf16[2,1,48,512]{3,2,0,1:T(8,128)(2,1)S(1)}, u32[]{:S(2)}, u32[]{:S(2)}) collective-permute-start(bf16[2,1,48,512]{3,2,0,1:T(8,128)(2,1)S(1)} %collective-permute-done.5), channel_id=1, source_target_pairs={{0,1},{1,2},{2,3},{3,4},{4,5},{5,6},{6,7},{7,8},{8,9},{9,10},{10,1... | collective-permute-start | bytes 294920 | tf_op jit(solution)/shard_map/ppermute | solution.py:17
  114.7 6.9 %collective-permute-start.13 = (bf16[2,1,48,512]{3,2,0,1:T(8,128)(2,1)S(1)}, bf16[2,1,48,512]{3,2,0,1:T(8,128)(2,1)S(1)}, u32[]{:S(2)}, u32[]{:S(2)}) collective-permute-start(bf16[2,1,48,512]{3,2,0,1:T(8,128)(2,1)S(1)} %collective-permute-done.12), channel_id=1, source_target_pairs={{0,15},{1,0},{2,1},{3,2},{4,3},{5,4},{6,5},{7,6},{8,7},{9,8},{10,9... | collective-permute-start | bytes 294920 | tf_op jit(solution)/shard_map/ppermute | solution.py:19
  121.6 6.7 %collective-permute-start.7 = (bf16[2,1,48,512]{3,2,0,1:T(8,128)(2,1)S(1)}, bf16[2,1,48,512]{3,2,0,1:T(8,128)(2,1)S(1)}, u32[]{:S(2)}, u32[]{:S(2)}) collective-permute-start(bf16[2,1,48,512]{3,2,0,1:T(8,128)(2,1)S(1)} %collective-permute-done.6), channel_id=1, source_target_pairs={{0,1},{1,2},{2,3},{3,4},{4,5},{5,6},{6,7},{7,8},{8,9},{9,10},{10,1... | collective-permute-start | bytes 294920 | tf_op jit(solution)/shard_map/ppermute | solution.py:17
  121.6 6.7 %collective-permute-start.14 = (bf16[2,1,48,512]{3,2,0,1:T(8,128)(2,1)S(1)}, bf16[2,1,48,512]{3,2,0,1:T(8,128)(2,1)S(1)}, u32[]{:S(2)}, u32[]{:S(2)}) collective-permute-start(bf16[2,1,48,512]{3,2,0,1:T(8,128)(2,1)S(1)} %collective-permute-done.13), channel_id=1, source_target_pairs={{0,15},{1,0},{2,1},{3,2},{4,3},{5,4},{6,5},{7,6},{8,7},{9,8},{10,9... | collective-permute-start | bytes 294920 | tf_op jit(solution)/shard_map/ppermute | solution.py:19
  128.3 6.8 %collective-permute-start.8 = (bf16[2,1,48,512]{3,2,0,1:T(8,128)(2,1)S(1)}, bf16[2,1,48,512]{3,2,0,1:T(8,128)(2,1)S(1)}, u32[]{:S(2)}, u32[]{:S(2)}) collective-permute-start(bf16[2,1,48,512]{3,2,0,1:T(8,128)(2,1)S(1)} %collective-permute-done.7), channel_id=1, source_target_pairs={{0,1},{1,2},{2,3},{3,4},{4,5},{5,6},{6,7},{7,8},{8,9},{9,10},{10,1... | collective-permute-start | bytes 294920 | tf_op jit(solution)/shard_map/ppermute | solution.py:17
  128.3 8.6 %collective-permute-start.15 = (bf16[2,1,48,512]{3,2,0,1:T(8,128)(2,1)S(1)}, bf16[2,1,48,512]{3,2,0,1:T(8,128)(2,1)S(1)}, u32[]{:S(2)}, u32[]{:S(2)}) collective-permute-start(bf16[2,1,48,512]{3,2,0,1:T(8,128)(2,1)S(1)} %collective-permute-done.14), channel_id=1, source_target_pairs={{0,15},{1,0},{2,1},{3,2},{4,3},{5,4},{6,5},{7,6},{8,7},{9,8},{10,9... | collective-permute-start | bytes 294920 | tf_op jit(solution)/shard_map/ppermute | solution.py:19
  135.2 9.0 %collective-permute-start.9 = (bf16[2,1,48,512]{3,2,0,1:T(8,128)(2,1)S(1)}, bf16[2,1,48,512]{3,2,0,1:T(8,128)(2,1)S(1)}, u32[]{:S(2)}, u32[]{:S(2)}) collective-permute-start(bf16[2,1,48,512]{3,2,0,1:T(8,128)(2,1)S(1)} %collective-permute-done.8), channel_id=1, source_target_pairs={{0,1},{1,2},{2,3},{3,4},{4,5},{5,6},{6,7},{7,8},{8,9},{9,10},{10,1... | collective-permute-start | bytes 294920 | tf_op jit(solution)/shard_map/ppermute | solution.py:17
  137.0 9.0 %collective-permute-start.16 = (bf16[2,1,48,512]{3,2,0,1:T(8,128)(2,1)S(1)}, bf16[2,1,48,512]{3,2,0,1:T(8,128)(2,1)S(1)}, u32[]{:S(2)}, u32[]{:S(2)}) collective-permute-start(bf16[2,1,48,512]{3,2,0,1:T(8,128)(2,1)S(1)} %collective-permute-done.15), channel_id=1, source_target_pairs={{0,15},{1,0},{2,1},{3,2},{4,3},{5,4},{6,5},{7,6},{8,7},{9,8},{10,9... | collective-permute-start | bytes 294920 | tf_op jit(solution)/shard_map/ppermute | solution.py:19
  149.9 4.6 %collective-permute-start.18 = (bf16[2,1,96,512]{3,2,0,1:T(8,128)(2,1)S(1)}, bf16[2,1,96,512]{3,2,0,1:T(8,128)(2,1)S(1)}, u32[]{:S(2)}, u32[]{:S(2)}) collective-permute-start(bf16[2,1,96,512]{3,2,0,1:T(8,128)(2,1)S(1)} %slice.314), channel_id=1, source_target_pairs={{1,0},{2,1},{3,2},{4,3},{5,4},{6,5},{7,6},{8,7},{9,8},{10,9},{11,1... | collective-permute-start | bytes 589832 | tf_op jit(solution)/shard_map/ppermute | solution.py:34
  151.2 4.1 %collective-permute-start.17 = (bf16[2,1,96,512]{3,2,0,1:T(8,128)(2,1)S(1)}, bf16[2,1,96,512]{3,2,0,1:T(8,128)(2,1)S(1)}, u32[]{:S(2)}, u32[]{:S(2)}) collective-permute-start(bf16[2,1,96,512]{3,2,0,1:T(8,128)(2,1)S(1)} %slice.314), channel_id=1, source_target_pairs={{0,1},{1,2},{2,3},{3,4},{4,5},{5,6},{6,7},{7,8},{8,9},{9,10},{10,1... | collective-permute-start | bytes 589832 | tf_op jit(solution)/shard_map/ppermute | solution.py:32
  (16 other events, 97.2 us)
Sparse Core Ops, SparseCore 0:
  84.0 38.9 all-gather.2
  125.1 111.0 all-gather.4
